TPU v7x, 512 devices: a whole 4x8x8 slice. The times are simulated.
512 devices in a mesh: leaf: 64 (over y, x, core), panel: 8 (over z).
Axes of the slice: x: 4, y: 8, z: 8, core: 2. Of those that a mesh axis runs over, the one named last changes fastest.
Arguments:
- rhs_0: bfloat16 [4096, 1024], P('leaf', 'panel'), may hold values from -6 to 6
- rhs_1: bfloat16 [4096, 1024], P('leaf', 'panel'), may hold values from -6 to 6
- rhs_2: bfloat16 [4096, 1024], P('leaf', 'panel'), may hold values from -6 to 6
- rhs_3: bfloat16 [4096, 1024], P('leaf', 'panel'), may hold values from -6 to 6
- inv_0: bfloat16 [4096, 4096], P(('leaf', 'panel')), as said below
- inv_1: bfloat16 [4096, 2048], P(('leaf', 'panel')), as said below
- inv_2: bfloat16 [4096, 1024], P(('leaf', 'panel')), as said below
- inv_3: bfloat16 [4096, 512], P(('leaf', 'panel')), as said below
- coupling_1: bfloat16 [4096, 2048], P(('leaf', 'panel')), may hold values from -0.125 to 0.125
- coupling_2: bfloat16 [4096, 1024], P(('leaf', 'panel')), may hold values from -0.1875 to 0.1875
- coupling_3: bfloat16 [4096, 512], P(('leaf', 'panel')), may hold values from -0.25 to 0.25
- update_rows_1: int32 [2, 2048], replicated, may hold values from 0 to 4095, as said below
- update_rows_2: int32 [4, 1024], replicated, may hold values from 0 to 6143, as said below
- update_rows_3: int32 [8, 512], replicated, may hold values from 0 to 7167, as said below
Outputs:
- solution_0: bfloat16 [4096, 1024], P('leaf', 'panel')
- solution_1: bfloat16 [4096, 1024], P('leaf', 'panel')
- solution_2: bfloat16 [4096, 1024], P('leaf', 'panel')
- solution_3: bfloat16 [4096, 1024], P('leaf', 'panel')
Inputs may be any that keep to these rules, and one draw needn't show every extreme that they name: `update_rows_1`: row f lists the update rows of front f of depth 1: 2048 distinct indices into its ancestor rows, holding 0 and the last ancestor row. `update_rows_2`: row f lists the update rows of front f of depth 2: 1024 distinct indices into its ancestor rows, holding 0 and the last ancestor row. `update_rows_3`: row f lists the update rows of front f of depth 3: 512 distinct indices into its ancestor rows, holding 0 and the last ancestor row. `inv_0`: the block is lower triangular with its diagonal between 0.5 and 2. `inv_1`: each 2048-row block is lower triangular with its diagonal between 0.5 and 2. `inv_2`: each 1024-row block is lower triangular with its diagonal between 0.5 and 2. `inv_3`: each 512-row block is lower triangular with its diagonal between 0.5 and 2.
All inputs are finite; a program needn't handle non-finite values.
Results may differ from a plain program's by a relative error of at most 0.014.
Values may be sent and summed in bfloat16 or wider, within the bound.
No kernel may reach another device: no remote copies, remote signals or barrier semaphores. Data moves between devices by JAX's collectives and lax.ppermute only.
A program may use at most 64 MiB of HBM per device.

v0:
```python
import jax
import jax.numpy as jnp
from jax import lax
from jax.sharding import PartitionSpec as P

PIVOTS = 4096
LEVELS = 4


def swapped(value, axis, bit):
    mask = 2**bit
    pairs = [(source, source ^ mask) for source in range(lax.axis_size(axis))]
    return lax.ppermute(value, axis, pairs)


def collect_rows(own_block, groups, front_rows):
    gathered = lax.all_gather(own_block, "leaf", axis=0, tiled=True)
    row_start = lax.axis_index("leaf") // groups * front_rows
    return lax.dynamic_slice_in_dim(gathered, row_start, front_rows, 0)


def halve_sums(block, groups):
    my_index = lax.axis_index("leaf")
    for bit_pos in reversed(range(groups.bit_length() - 1)):
        half_rows = block.shape[0] // 2
        lower_half = block[:half_rows]
        upper_half = block[half_rows:]
        is_high = my_index >> bit_pos & 1 == 1
        keep_part = jnp.where(is_high, upper_half, lower_half)
        send_part = jnp.where(is_high, lower_half, upper_half)
        block = keep_part + swapped(send_part, "leaf", bit_pos)
    return block


def reduce_rows(block, groups):
    return halve_sums(block, groups)


def contract_rows(left, right):
    return lax.dot_general(
        left, right, (((0,), (0,)), ((), ())), preferred_element_type=jnp.float32
    )


def body(
    rhs_0,
    rhs_1,
    rhs_2,
    rhs_3,
    inv_0,
    inv_1,
    inv_2,
    inv_3,
    coupling_1,
    coupling_2,
    coupling_3,
    update_rows_1,
    update_rows_2,
    update_rows_3,
):
    rhs_all = [rhs_0, rhs_1, rhs_2, rhs_3]
    lists_all = [None, update_rows_1, update_rows_2, update_rows_3]
    columns = rhs_0.shape[1]
    leaf_count = lax.axis_size("leaf")
    front_sizes = [PIVOTS >> depth_now for depth_now in range(LEVELS)]
    offsets = [0]
    for depth_now in range(1, LEVELS):
        offsets.append(offsets[-1] + front_sizes[depth_now - 1])
    fetched = (
        lax.all_gather(inv_0, "panel", axis=0, tiled=True),
        lax.all_gather(inv_1, "panel", axis=0, tiled=True),
        lax.all_gather(inv_2, "panel", axis=0, tiled=True),
        lax.all_gather(inv_3, "panel", axis=0, tiled=True),
        lax.all_gather(coupling_1, "panel", axis=0, tiled=True),
        lax.all_gather(coupling_2, "panel", axis=0, tiled=True),
        lax.all_gather(coupling_3, "panel", axis=0, tiled=True),
    )
    inv_rows_all = [fetched[0], fetched[1], fetched[2], fetched[3]]
    coup_rows_all = [None, fetched[4], fetched[5], fetched[6]]
    accumulated = jnp.zeros((offsets[LEVELS - 1], columns), jnp.float32)
    forwards = [None] * LEVELS
    for depth_now in reversed(range(LEVELS)):
        groups = leaf_count >> depth_now
        front_rows = front_sizes[depth_now]
        front = lax.axis_index("leaf") // groups
        summed = rhs_all[depth_now].astype(jnp.float32)
        if depth_now < LEVELS - 1:
            summed = summed + reduce_rows(
                accumulated[offsets[depth_now] : offsets[depth_now] + front_rows], groups
            )
        combined = collect_rows(summed.astype(jnp.bfloat16), groups, front_rows)
        values = jnp.dot(
            inv_rows_all[depth_now], combined, preferred_element_type=jnp.float32
        ).astype(jnp.bfloat16)
        forwards[depth_now] = values
        if depth_now > 0:
            update = contract_rows(coup_rows_all[depth_now], values)
            row_list = lax.dynamic_index_in_dim(lists_all[depth_now], front, 0, keepdims=False)
            accumulated = accumulated.at[row_list].add(update)
    anc_values = jnp.zeros((offsets[LEVELS - 1], columns), jnp.bfloat16)
    outputs = []
    for depth_now in range(LEVELS):
        groups = leaf_count >> depth_now
        front_rows = front_sizes[depth_now]
        front = lax.axis_index("leaf") // groups
        if depth_now > 0:
            row_list = lax.dynamic_index_in_dim(lists_all[depth_now], front, 0, keepdims=False)
            picked = jnp.take(anc_values, row_list, axis=0)
            pulled = jnp.dot(coup_rows_all[depth_now], picked, preferred_element_type=jnp.float32)
            adjusted = (forwards[depth_now].astype(jnp.float32) - pulled).astype(jnp.bfloat16)
        else:
            adjusted = forwards[depth_now]
        partial_value = contract_rows(inv_rows_all[depth_now], adjusted)
        solved = reduce_rows(partial_value, groups).astype(jnp.bfloat16)
        outputs.append(solved)
        if depth_now < LEVELS - 1:
            whole_front = collect_rows(solved, groups, front_rows)
            anc_values = anc_values.at[offsets[depth_now] : offsets[depth_now] + front_rows].set(
                whole_front
            )
    return (outputs[0], outputs[1], outputs[2], outputs[3])


def solution(mesh):
    in_specs = (
        P("leaf", "panel"),
        P("leaf", "panel"),
        P("leaf", "panel"),
        P("leaf", "panel"),
        P(("leaf", "panel"), None),
        P(("leaf", "panel"), None),
        P(("leaf", "panel"), None),
        P(("leaf", "panel"), None),
        P(("leaf", "panel"), None),
        P(("leaf", "panel"), None),
        P(("leaf", "panel"), None),
        P(),
        P(),
        P(),
    )
    out_specs = (P("leaf", "panel"), P("leaf", "panel"), P("leaf", "panel"), P("leaf", "panel"))
    return jax.shard_map(body, mesh=mesh, in_specs=in_specs, out_specs=out_specs, check_vma=False)
```

profile of v0, /device:TPU:1, one launch (start us, length us, event | category | flops | bytes accessed | tf_op | source)
XLA Modules:
  0.0 1056.7 jit_solution(4610110368345489924)
XLA Ops:
  8.0 25.9 %all_gather.43 = bf16[64,512]{1,0:T(8,128)(2,1)S(1)} all-gather(bf16[8,512]{1,0:T(8,128)(2,1)} %param.27), channel_id=1, replica_groups=mesh['leaf'=64,'panel'=8] {'panel'}, dimensions={0}, use_global_device_ids=true | all-gather | bytes 73728 | tf_op jit(solution)/shard_map/all_gather | solution.py:73
  33.9 19.2 %all_gather.44 = bf16[64,512]{1,0:T(8,128)(2,1)S(1)} all-gather(bf16[8,512]{1,0:T(8,128)(2,1)} %param.30), channel_id=1, replica_groups=mesh['leaf'=64,'panel'=8] {'panel'}, dimensions={0}, use_global_device_ids=true | all-gather | bytes 73728 | tf_op jit(solution)/shard_map/all_gather | solution.py:76
  54.4 44.7 %all-gather.8.cloned.1.call-done = bf16[4096,128]{1,0:T(8,128)(2,1)} async-done(((bf16[64,128]{1,0:T(8,128)(2,1)}), bf16[4096,128]{1,0:T(8,128)(2,1)}) %all-gather.8.cloned.1.call-update) | async-done | bytes 1048592 | tf_op jit(solution)/shard_map/all_gather | solution.py:17
  101.2 4.2 scatter_custom_fusion
  108.7 7.2 collective-permute-done
  117.1 3.7 collective-permute-start.1
  129.4 5.4 collective-permute-start.3
  136.3 20.5 %all_gather.46 = bf16[64,1024]{1,0:T(8,128)(2,1)S(1)} all-gather(bf16[8,1024]{1,0:T(8,128)(2,1)S(1)} %copy-done.13), channel_id=1, replica_groups=mesh['leaf'=64,'panel'=8] {'panel'}, dimensions={0}, use_global_device_ids=true | all-gather | bytes 147456 | tf_op jit(solution)/shard_map/all_gather | solution.py:72
  156.8 19.3 %all_gather.47 = bf16[64,1024]{1,0:T(8,128)(2,1)S(1)} all-gather(bf16[8,1024]{1,0:T(8,128)(2,1)S(1)} %copy-done.14), channel_id=1, replica_groups=mesh['leaf'=64,'panel'=8] {'panel'}, dimensions={0}, use_global_device_ids=true | all-gather | bytes 147456 | tf_op jit(solution)/shard_map/all_gather | solution.py:75
  177.4 39.1 %all-gather.10.cloned.1.call-done = bf16[4096,128]{1,0:T(8,128)(2,1)} async-done(((bf16[64,128]{1,0:T(8,128)(2,1)}), bf16[4096,128]{1,0:T(8,128)(2,1)}) %all-gather.10.cloned.1.call-update) | async-done | bytes 1048592 | tf_op jit(solution)/shard_map/all_gather | solution.py:17
  218.1 9.3 scatter_fusion
  228.7 3.9 collective-permute-start.4
  232.6 23.9 %collective-permute-done.4 = f32[1024,128]{1,0:T(8,128)S(1)} collective-permute-done((f32[1024,128]{1,0:T(8,128)S(1)}, f32[1024,128]{1,0:T(8,128)S(1)}, u32[]{:S(2)}, u32[]{:S(2)}) %collective-permute-start.4) | collective-permute-done | bytes 524320 | tf_op jit(solution)/shard_map/ppermute | solution.py:13
  259.8 7.3 collective-permute-done.5
  269.9 4.5 collective-permute-done.6
  279.5 5.6 collective-permute-start.8
  286.6 20.6 %all_gather.49 = bf16[64,2048]{1,0:T(8,128)(2,1)S(1)} all-gather(bf16[8,2048]{1,0:T(8,128)(2,1)S(1)} %copy-done.11), channel_id=1, replica_groups=mesh['leaf'=64,'panel'=8] {'panel'}, dimensions={0}, use_global_device_ids=true | all-gather | bytes 294912 | tf_op jit(solution)/shard_map/all_gather | solution.py:71
  307.3 20.0 %all_gather.50 = bf16[64,2048]{1,0:T(8,128)(2,1)S(1)} all-gather(bf16[8,2048]{1,0:T(8,128)(2,1)S(1)} %copy-done.12), channel_id=1, replica_groups=mesh['leaf'=64,'panel'=8] {'panel'}, dimensions={0}, use_global_device_ids=true | all-gather | bytes 294912 | tf_op jit(solution)/shard_map/all_gather | solution.py:74
  327.3 39.1 %all-gather.12.cloned.1.call-done = bf16[4096,128]{1,0:T(8,128)(2,1)} async-done(((bf16[64,128]{1,0:T(8,128)(2,1)}), bf16[4096,128]{1,0:T(8,128)(2,1)}) %all-gather.12.cloned.1.call-update) | async-done | bytes 1048592 | tf_op jit(solution)/shard_map/all_gather | solution.py:17
  368.3 14.2 %scatter_fusion.1 = f32[7168,128]{1,0:T(8,128)} fusion(f32[7168,128]{1,0:T(8,128)} %scatter_fusion, s32[2048]{0:T(1024)S(1)} %bitcast.44, f32[2048,128]{1,0:T(8,128)S(1)} %copy.80), kind=kCustom, calls=%fused_computation.5 | custom fusion | flops 262144 | bytes 3153920 | tf_op jit(solution)/shard_map/scatter-add | solution.py:99
  384.1 4.9 collective-permute-start.9
  388.9 32.4 %collective-permute-done.9 = f32[2048,128]{1,0:T(8,128)S(1)} collective-permute-done((f32[2048,128]{1,0:T(8,128)S(1)}, f32[2048,128]{1,0:T(8,128)S(1)}, u32[]{:S(2)}, u32[]{:S(2)}) %collective-permute-start.9) | collective-permute-done | bytes 1048608 | tf_op jit(solution)/shard_map/ppermute | solution.py:13
  423.1 19.9 %collective-permute-start.10 = (f32[1024,128]{1,0:T(8,128)S(1)}, f32[1024,128]{1,0:T(8,128)S(1)}, u32[]{:S(2)}, u32[]{:S(2)}) collective-permute-start(f32[1024,128]{1,0:T(8,128)S(1)} %slice_select_fusion.4), channel_id=1, source_target_pairs={{0,128},{8,136},{16,144},{24,152},{32,160},{40,168},{48,176},{56,1... | collective-permute-start | bytes 1572872 | tf_op jit(solution)/shard_map/ppermute | solution.py:13
  443.1 23.3 %collective-permute-done.10 = f32[1024,128]{1,0:T(8,128)S(1)} collective-permute-done((f32[1024,128]{1,0:T(8,128)S(1)}, f32[1024,128]{1,0:T(8,128)S(1)}, u32[]{:S(2)}, u32[]{:S(2)}) %collective-permute-start.10) | collective-permute-done | bytes 524320 | tf_op jit(solution)/shard_map/ppermute | solution.py:13
  468.4 7.4 collective-permute-done.11
  488.2 5.5 collective-permute-start.14
  495.3 22.4 %all_gather.52 = bf16[64,4096]{1,0:T(8,128)(2,1)S(1)} all-gather(bf16[8,4096]{1,0:T(8,128)(2,1)S(1)} %copy-done.9), channel_id=1, replica_groups=mesh['leaf'=64,'panel'=8] {'panel'}, dimensions={0}, use_global_device_ids=true | all-gather | bytes 589824 | tf_op jit(solution)/shard_map/all_gather | solution.py:70
  517.7 57.2 %all-gather.14.cloned.1.call-done = bf16[4096,128]{1,0:T(8,128)(2,1)} async-done(((bf16[64,128]{1,0:T(8,128)(2,1)}), bf16[4096,128]{1,0:T(8,128)(2,1)}) %all-gather.14.cloned.1.call-update) | async-done | bytes 1048592 | tf_op jit(solution)/shard_map/all_gather | solution.py:17
  577.0 4.9 collective-permute-start.15
  581.9 32.4 %collective-permute-done.15 = f32[2048,128]{1,0:T(8,128)S(1)} collective-permute-done((f32[2048,128]{1,0:T(8,128)S(1)}, f32[2048,128]{1,0:T(8,128)S(1)}, u32[]{:S(2)}, u32[]{:S(2)}) %collective-permute-start.15) | collective-permute-done | bytes 1048608 | tf_op jit(solution)/shard_map/ppermute | solution.py:13
  614.5 19.9 %collective-permute-start.16 = (f32[1024,128]{1,0:T(8,128)S(1)}, f32[1024,128]{1,0:T(8,128)S(1)}, u32[]{:S(2)}, u32[]{:S(2)}) collective-permute-start(f32[1024,128]{1,0:T(8,128)S(1)} %slice_select_fusion.3), channel_id=1, source_target_pairs={{0,128},{8,136},{16,144},{24,152},{32,160},{40,168},{48,176},{56,1... | collective-permute-start | bytes 1572872 | tf_op jit(solution)/shard_map/ppermute | solution.py:13
  634.4 23.3 %collective-permute-done.16 = f32[1024,128]{1,0:T(8,128)S(1)} collective-permute-done((f32[1024,128]{1,0:T(8,128)S(1)}, f32[1024,128]{1,0:T(8,128)S(1)}, u32[]{:S(2)}, u32[]{:S(2)}) %collective-permute-start.16) | collective-permute-done | bytes 524320 | tf_op jit(solution)/shard_map/ppermute | solution.py:13
  659.8 7.4 collective-permute-done.17
  679.6 5.5 collective-permute-start.20
  687.2 79.0 %all-gather.16.cloned.1.call-done = bf16[4096,128]{1,0:T(8,128)(2,1)} async-done(((bf16[64,128]{1,0:T(8,128)(2,1)}), bf16[4096,128]{1,0:T(8,128)(2,1)}) %all-gather.16.cloned.1.call-update) | async-done | bytes 1048592 | tf_op jit(solution)/shard_map/all_gather | solution.py:17
  767.7 8.0 gather_fusion
  777.6 3.9 collective-permute-start.21
  781.5 23.9 %collective-permute-done.21 = f32[1024,128]{1,0:T(8,128)S(1)} collective-permute-done((f32[1024,128]{1,0:T(8,128)S(1)}, f32[1024,128]{1,0:T(8,128)S(1)}, u32[]{:S(2)}, u32[]{:S(2)}) %collective-permute-start.21) | collective-permute-done | bytes 524320 | tf_op jit(solution)/shard_map/ppermute | solution.py:13
  807.6 7.3 collective-permute-done.22
  817.7 4.5 collective-permute-done.23
  827.3 5.6 collective-permute-start.25
  835.8 78.3 %all-gather.18.cloned.1.call-done = bf16[4096,128]{1,0:T(8,128)(2,1)} async-done(((bf16[64,128]{1,0:T(8,128)(2,1)}), bf16[4096,128]{1,0:T(8,128)(2,1)}) %all-gather.18.cloned.1.call-update) | async-done | bytes 1048592 | tf_op jit(solution)/shard_map/all_gather | solution.py:17
  921.4 7.2 collective-permute-done.26
  941.0 5.4 collective-permute-start.29
  947.8 80.3 %all-gather.20.cloned.1.call-done = bf16[4096,128]{1,0:T(8,128)(2,1)} async-done(((bf16[64,128]{1,0:T(8,128)(2,1)}), bf16[4096,128]{1,0:T(8,128)(2,1)}) %all-gather.20.cloned.1.call-update) | async-done | bytes 1048592 | tf_op jit(solution)/shard_map/all_gather | solution.py:17
  1030.9 3.7 collective-permute-start.30
  1034.7 4.4 collective-permute-done.30
  1044.2 4.2 collective-permute-start.32
  (187 shorter events, 121.6 us)
Async XLA Ops:
  7.2 92.0 %all-gather.8.cloned.1.call-start = ((), (), s32[]{:S(2)}) async-start(), calls=%async_computation | async-start | bytes 1064960 | tf_op jit(solution)/shard_map/all_gather | solution.py:17
  7.9 208.6 %all-gather.10.cloned.1.call-start = ((), (), s32[]{:S(2)}) async-start(), calls=%async_computation.1 | async-start | bytes 1064960 | tf_op jit(solution)/shard_map/all_gather | solution.py:17
  33.9 86.9 %copy-start.2 = (bf16[64,512]{1,0:T(8,128)(2,1)}, bf16[64,512]{1,0:T(8,128)(2,1)S(1)}, u32[]{:S(2)}) copy-start(bf16[64,512]{1,0:T(8,128)(2,1)S(1)} %all_gather.43) | copy-start | bytes 196612
  106.5 9.5 collective-permute-start
  117.1 7.2 collective-permute-start.1
  124.3 5.0 collective-permute-start.2
  129.4 6.2 collective-permute-start.3
  136.2 230.1 %all-gather.12.cloned.1.call-start = ((), (), s32[]{:S(2)}) async-start(), calls=%async_computation.2 | async-start | bytes 1064960 | tf_op jit(solution)/shard_map/all_gather | solution.py:17
  227.4 79.9 %copy-start.12 = (bf16[8,2048]{1,0:T(8,128)(2,1)S(1)}, bf16[8,2048]{1,0:T(8,128)(2,1)}, u32[]{:S(2)}) copy-start(bf16[8,2048]{1,0:T(8,128)(2,1)} %param.28) | copy-start | bytes 98308
  227.4 99.8 %copy-start.21 = (s32[2,2048]{1,0:T(2,128)S(1)}, s32[2,2048]{1,0:T(2,128)}, u32[]{:S(2)}) copy-start(s32[2,2048]{1,0:T(2,128)} %param.31) | copy-start | bytes 49156
  228.7 27.8 %collective-permute-start.4 = (f32[1024,128]{1,0:T(8,128)S(1)}, f32[1024,128]{1,0:T(8,128)S(1)}, u32[]{:S(2)}, u32[]{:S(2)}) collective-permute-start(f32[1024,128]{1,0:T(8,128)S(1)} %slice_select_fusion.5), channel_id=1, source_target_pairs={{0,128},{8,136},{16,144},{24,152},{32,160},{40,168},{48,176},{56,1... | collective-permute-start | bytes 1572872 | tf_op jit(solution)/shard_map/ppermute | solution.py:13
  257.9 9.2 collective-permute-start.5
  267.2 7.2 collective-permute-start.6
  274.5 5.0 collective-permute-start.7
  279.5 6.4 collective-permute-start.8
  286.6 288.4 %all-gather.14.cloned.1.call-start = ((), (), s32[]{:S(2)}) async-start(), calls=%async_computation.3 | async-start | bytes 1064960 | tf_op jit(solution)/shard_map/all_gather | solution.py:17
  384.1 37.3 %collective-permute-start.9 = (f32[2048,128]{1,0:T(8,128)S(1)}, f32[2048,128]{1,0:T(8,128)S(1)}, u32[]{:S(2)}, u32[]{:S(2)}) collective-permute-start(f32[2048,128]{1,0:T(8,128)S(1)} %slice_select_fusion.1), channel_id=1, source_target_pairs={{0,256},{8,264},{16,272},{24,280},{32,288},{40,296},{48,304},{56,3... | collective-permute-start | bytes 3145736 | tf_op jit(solution)/shard_map/ppermute | solution.py:13
  423.0 72.2 %copy-start.9 = (bf16[8,4096]{1,0:T(8,128)(2,1)S(1)}, bf16[8,4096]{1,0:T(8,128)(2,1)}, u32[]{:S(2)}) copy-start(bf16[8,4096]{1,0:T(8,128)(2,1)} %param.24) | copy-start | bytes 196612
  423.1 43.3 %collective-permute-start.10 = (f32[1024,128]{1,0:T(8,128)S(1)}, f32[1024,128]{1,0:T(8,128)S(1)}, u32[]{:S(2)}, u32[]{:S(2)}) collective-permute-start(f32[1024,128]{1,0:T(8,128)S(1)} %slice_select_fusion.4), channel_id=1, source_target_pairs={{0,128},{8,136},{16,144},{24,152},{32,160},{40,168},{48,176},{56,1... | collective-permute-start | bytes 1572872 | tf_op jit(solution)/shard_map/ppermute | solution.py:13
  466.5 9.3 collective-permute-start.11
  475.9 7.2 collective-permute-start.12
  483.1 5.0 collective-permute-start.13
  488.2 6.4 collective-permute-start.14
  495.2 271.0 %all-gather.16.cloned.1.call-start = ((), (), s32[]{:S(2)}) async-start(), calls=%async_computation.4 | async-start | bytes 1064960 | tf_op jit(solution)/shard_map/all_gather | solution.py:17
  577.0 37.3 %collective-permute-start.15 = (f32[2048,128]{1,0:T(8,128)S(1)}, f32[2048,128]{1,0:T(8,128)S(1)}, u32[]{:S(2)}, u32[]{:S(2)}) collective-permute-start(f32[2048,128]{1,0:T(8,128)S(1)} %slice_select_fusion), channel_id=1, source_target_pairs={{0,256},{8,264},{16,272},{24,280},{32,288},{40,296},{48,304},{56,3... | collective-permute-start | bytes 3145736 | tf_op jit(solution)/shard_map/ppermute | solution.py:13
  614.5 43.3 %collective-permute-start.16 = (f32[1024,128]{1,0:T(8,128)S(1)}, f32[1024,128]{1,0:T(8,128)S(1)}, u32[]{:S(2)}, u32[]{:S(2)}) collective-permute-start(f32[1024,128]{1,0:T(8,128)S(1)} %slice_select_fusion.3), channel_id=1, source_target_pairs={{0,128},{8,136},{16,144},{24,152},{32,160},{40,168},{48,176},{56,1... | collective-permute-start | bytes 1572872 | tf_op jit(solution)/shard_map/ppermute | solution.py:13
  657.9 9.3 collective-permute-start.17
  667.3 7.2 collective-permute-start.18
  674.5 5.0 collective-permute-start.19
  679.6 6.4 collective-permute-start.20
  686.6 227.5 %all-gather.18.cloned.1.call-start = ((), (), s32[]{:S(2)}) async-start(), calls=%async_computation.5 | async-start | bytes 1064960 | tf_op jit(solution)/shard_map/all_gather | solution.py:17
  777.6 27.8 %collective-permute-start.21 = (f32[1024,128]{1,0:T(8,128)S(1)}, f32[1024,128]{1,0:T(8,128)S(1)}, u32[]{:S(2)}, u32[]{:S(2)}) collective-permute-start(f32[1024,128]{1,0:T(8,128)S(1)} %slice_select_fusion.2), channel_id=1, source_target_pairs={{0,128},{8,136},{16,144},{24,152},{32,160},{40,168},{48,176},{56,1... | collective-permute-start | bytes 1572872 | tf_op jit(solution)/shard_map/ppermute | solution.py:13
  805.5 113.0 %copy-start.1 = (bf16[64,1024]{1,0:T(8,128)(2,1)S(1)}, bf16[64,1024]{1,0:T(8,128)(2,1)}, u32[]{:S(2)}) copy-start(bf16[64,1024]{1,0:T(8,128)(2,1)} %copy-done) | copy-start | bytes 393220
  805.5 9.4 collective-permute-start.22
  815.0 7.2 collective-permute-start.23
  822.2 5.0 collective-permute-start.24
  827.3 6.4 collective-permute-start.25
  834.4 193.8 %all-gather.20.cloned.1.call-start = ((), (), s32[]{:S(2)}) async-start(), calls=%async_computation.6 | async-start | bytes 1064960 | tf_op jit(solution)/shard_map/all_gather | solution.py:17
  918.5 112.0 %copy-start.3 = (bf16[64,512]{1,0:T(8,128)(2,1)S(1)}, bf16[64,512]{1,0:T(8,128)(2,1)}, u32[]{:S(2)}) copy-start(bf16[64,512]{1,0:T(8,128)(2,1)} %copy-done.2) | copy-start | bytes 196612
  918.5 112.0 %copy-start.5 = (bf16[64,512]{1,0:T(8,128)(2,1)S(1)}, bf16[64,512]{1,0:T(8,128)(2,1)}, u32[]{:S(2)}) copy-start(bf16[64,512]{1,0:T(8,128)(2,1)} %copy-done.4) | copy-start | bytes 196612
  918.5 112.0 %copy-start.8 = (bf16[128,64]{0,1:T(8,128)(2,1)S(1)}, bf16[128,64]{0,1:T(8,128)(2,1)}, u32[]{:S(2)}) copy-start(bf16[128,64]{0,1:T(8,128)(2,1)} %copy-done.7) | copy-start | bytes 49156
  919.1 9.5 collective-permute-start.26
  928.7 7.2 collective-permute-start.27
  935.9 5.0 collective-permute-start.28
  941.0 6.2 collective-permute-start.29
  1030.9 8.2 collective-permute-start.30
  1039.2 5.0 collective-permute-start.31
  1044.2 5.0 collective-permute-start.32
  (14 other events, 624.3 us)
Sparse Core Ops, SparseCore 0:
  11.3 87.8 all-gather.7
  136.4 80.1 all-gather.9
  286.7 79.5 all-gather.11
  495.3 79.5 all-gather.13
  686.7 79.4 all-gather.15
  834.5 79.6 all-gather.17
  947.9 80.1 all-gather.19
where the time goes:
time: 1060 us
  waiting for transfers between devices  676 us (64%)
  blocking collectives  148 us (14%)
  starting transfers between devices  145 us (14%)
  other arithmetic  46.2 us (4%)
  local copies, waits for them, and re-layouts  17.4 us (2%)
  between operations  15.2 us (1%)
    all_gather x7, waiting for transfers between devices, collect_rows(): gathered = lax.all_gather(own_block, 'leaf', axis=0, tiled=True)  418 us
    ppermute x33, waiting for transfers between devices, swapped(): return lax.ppermute(value, axis, pairs)  257 us
    ppermute x33, starting transfers between devices, swapped(): return lax.ppermute(value, axis, pairs)  145 us
    scatter-add x3, other arithmetic, body(): accumulated = accumulated.at[row_list].add(update)  27.6 us
    all_gather x1, blocking collectives, body(): lax.all_gather(inv_3, 'panel', axis=0, tiled=True)  25.9 us
    all_gather x1, blocking collectives, body(): lax.all_gather(inv_0, 'panel', axis=0, tiled=True)  22.4 us
  transfers between devices with their start and end apart: 40, of which 40 were waited for; matrix products, arithmetic and copies ran while one was open for 0% of the time, Pallas kernels for 0%

commit v1 on v0

--- a/solution.py
+++ b/solution.py
@@ -14,7 +14,10 @@
 
 
 def collect_rows(own_block, groups, front_rows):
-    gathered = lax.all_gather(own_block, "leaf", axis=0, tiled=True)
+    peers = lax.axis_size("leaf")
+    blocks = jnp.stack([own_block for _ in range(peers)])
+    blocks = lax.all_to_all(blocks, "leaf", split_axis=0, concat_axis=0)
+    gathered = jnp.concatenate(blocks, axis=0)
     row_start = lax.axis_index("leaf") // groups * front_rows
     return lax.dynamic_slice_in_dim(gathered, row_start, front_rows, 0)
 

time: 1060 us -> 777 us (0.73)
  waiting for transfers between devices: 676 us -> 310 us
  starting transfers between devices: 145 us -> 238 us
  between operations: 15.2 us -> 1.72 us
    all_gather x7 -> x0, waiting for transfers between devices: 418 us -> none  [collect_rows(): gathered = lax.all_gather(own_block, 'leaf', axis=0, tiled=True)]
    all_to_all x0 -> x7, waiting for transfers between devices: none -> 87.5 us  [collect_rows(): blocks = lax.all_to_all(blocks, 'leaf', split_axis=0, concat_axis=0)]
    all_to_all x0 -> x7, starting transfers between devices: none -> 55.5 us  [collect_rows(): blocks = lax.all_to_all(blocks, 'leaf', split_axis=0, concat_axis=0)]
    ppermute x33, starting transfers between devices: 145 us -> 182 us  [swapped(): return lax.ppermute(value, axis, pairs)]
    ppermute x33, waiting for transfers between devices: 257 us -> 222 us  [swapped(): return lax.ppermute(value, axis, pairs)]
  transfers between devices with their start and end apart: 40 -> 40, of which waited for: 40 -> 37; matrix products, arithmetic and copies ran while one was open for 0% -> 1% of each run, Pallas kernels for 0% -> 0%
where the time goes in v1:
time: 777 us; the launch traced here: 775 us
  waiting for transfers between devices  310 us (40%)
  starting transfers between devices  238 us (31%)
  blocking collectives  148 us (19%)
  other arithmetic  44.2 us (6%)
  local copies, waits for them, and re-layouts  25.6 us (3%)
  matrix products  7.86 us (1%)
    ppermute x33, waiting for transfers between devices, swapped(): return lax.ppermute(value, axis, pairs)  222 us
    ppermute x33, starting transfers between devices, swapped(): return lax.ppermute(value, axis, pairs)  182 us
    all_to_all x7, waiting for transfers between devices, collect_rows(): blocks = lax.all_to_all(blocks, 'leaf', split_axis=0, concat_axis=0)  87.5 us
    all_to_all x7, starting transfers between devices, collect_rows(): blocks = lax.all_to_all(blocks, 'leaf', split_axis=0, concat_axis=0)  55.5 us
    scatter-add x3, other arithmetic, body(): accumulated = accumulated.at[row_list].add(update)  27.6 us
    all_gather x1, blocking collectives, body(): lax.all_gather(inv_3, 'panel', axis=0, tiled=True)  26.8 us
    all_gather x1, blocking collectives, body(): lax.all_gather(inv_0, 'panel', axis=0, tiled=True)  22 us
    all_gather x1, blocking collectives, body(): lax.all_gather(inv_1, 'panel', axis=0, tiled=True)  20.6 us
  transfers between devices with their start and end apart: 40, of which 37 were waited for; matrix products, arithmetic and copies ran while one was open for 1% of the time, Pallas kernels for 0%

profile of v1, /device:TPU:1, one launch (start us, length us, event | category | flops | bytes accessed | tf_op | source)
XLA Modules:
  0.0 774.8 jit_solution(14272911442897763930)
XLA Ops:
  2.6 11.6 %all-to-all-start = ((bf16[64,64,128]{2,1,0:T(8,128)(2,1)}), bf16[64,64,128]{2,1,0:T(8,128)(2,1)S(1)}, u32[]{:S(2)}, u32[]{:S(2)}) async-start(bf16[64,64,128]{2,1,0:T(8,128)(2,1)} %stack.14), calls=%async_computation | async-start | bytes 2097152 | tf_op jit(solution)/shard_map/all_to_all | solution.py:19
  14.3 26.8 %all_gather.21 = bf16[64,512]{1,0:T(8,128)(2,1)S(1)} all-gather(bf16[8,512]{1,0:T(8,128)(2,1)} %param.27), channel_id=1, replica_groups=mesh['leaf'=64,'panel'=8] {'panel'}, dimensions={0}, use_global_device_ids=true | all-gather | bytes 73728 | tf_op jit(solution)/shard_map/all_gather | solution.py:76
  41.0 19.0 %all_gather.22 = bf16[64,512]{1,0:T(8,128)(2,1)S(1)} all-gather(bf16[8,512]{1,0:T(8,128)(2,1)} %param.30), channel_id=1, replica_groups=mesh['leaf'=64,'panel'=8] {'panel'}, dimensions={0}, use_global_device_ids=true | all-gather | bytes 73728 | tf_op jit(solution)/shard_map/all_gather | solution.py:79
  76.0 4.4 collective-permute-start.1
  88.3 16.0 %collective-permute-start.3 = (f32[64,128]{1,0:T(8,128)S(1)}, f32[64,128]{1,0:T(8,128)S(1)}, u32[]{:S(2)}, u32[]{:S(2)}) collective-permute-start(f32[64,128]{1,0:T(8,128)S(1)} %slice_select_fusion.32), channel_id=1, source_target_pairs={{0,8},{8,0},{16,24},{24,16},{32,40},{40,32},{48,56},{56,48},{64,72... | collective-permute-start | bytes 98312 | tf_op jit(solution)/shard_map/ppermute | solution.py:13
  106.4 10.2 %all-to-all-start.1 = ((bf16[64,64,128]{2,1,0:T(8,128)(2,1)}), bf16[64,64,128]{2,1,0:T(8,128)(2,1)S(1)}, u32[]{:S(2)}, u32[]{:S(2)}) async-start(bf16[64,64,128]{2,1,0:T(8,128)(2,1)} %stack.15), calls=%async_computation.1 | async-start | bytes 2097152 | tf_op jit(solution)/shard_map/all_to_all | solution.py:19
  116.7 20.3 %all_gather.23 = bf16[64,1024]{1,0:T(8,128)(2,1)S(1)} all-gather(bf16[8,1024]{1,0:T(8,128)(2,1)S(1)} %copy-done.18), channel_id=1, replica_groups=mesh['leaf'=64,'panel'=8] {'panel'}, dimensions={0}, use_global_device_ids=true | all-gather | bytes 147456 | tf_op jit(solution)/shard_map/all_gather | solution.py:75
  137.0 19.1 %all_gather.24 = bf16[64,1024]{1,0:T(8,128)(2,1)S(1)} all-gather(bf16[8,1024]{1,0:T(8,128)(2,1)S(1)} %copy-done.19), channel_id=1, replica_groups=mesh['leaf'=64,'panel'=8] {'panel'}, dimensions={0}, use_global_device_ids=true | all-gather | bytes 147456 | tf_op jit(solution)/shard_map/all_gather | solution.py:78
  158.1 9.3 %scatter_fusion = f32[7168,128]{1,0:T(8,128)} fusion(f32[7168,128]{1,0:T(8,128)} %scatter_custom_fusion, s32[1024]{0:T(1024)S(1)} %bitcast.60, f32[1024,128]{1,0:T(8,128)S(1)} %copy.63), kind=kCustom, calls=%fused_computation.4 | custom fusion | flops 131072 | bytes 1576960 | tf_op jit(solution)/shard_map/scatter-add | solution.py:102
  172.7 18.8 %collective-permute-done.4 = f32[1024,128]{1,0:T(8,128)S(1)} collective-permute-done((f32[1024,128]{1,0:T(8,128)S(1)}, f32[1024,128]{1,0:T(8,128)S(1)}, u32[]{:S(2)}, u32[]{:S(2)}) %collective-permute-start.4) | collective-permute-done | bytes 524320 | tf_op jit(solution)/shard_map/ppermute | solution.py:13
  195.0 5.0 collective-permute-done.5
  200.1 4.9 collective-permute-start.6
  212.4 11.5 %collective-permute-start.8 = (f32[64,128]{1,0:T(8,128)S(1)}, f32[64,128]{1,0:T(8,128)S(1)}, u32[]{:S(2)}, u32[]{:S(2)}) collective-permute-start(f32[64,128]{1,0:T(8,128)S(1)} %slice_select_fusion.31), channel_id=1, source_target_pairs={{0,8},{8,0},{16,24},{24,16},{32,40},{40,32},{48,56},{56,48},{64,72... | collective-permute-start | bytes 98312 | tf_op jit(solution)/shard_map/ppermute | solution.py:13
  226.0 9.0 %all-to-all-start.2 = ((bf16[64,64,128]{2,1,0:T(8,128)(2,1)}), bf16[64,64,128]{2,1,0:T(8,128)(2,1)S(1)}, u32[]{:S(2)}, u32[]{:S(2)}) async-start(bf16[64,64,128]{2,1,0:T(8,128)(2,1)} %stack.16), calls=%async_computation.2 | async-start | bytes 2097152 | tf_op jit(solution)/shard_map/all_to_all | solution.py:19
  235.1 20.6 %all_gather.25 = bf16[64,2048]{1,0:T(8,128)(2,1)S(1)} all-gather(bf16[8,2048]{1,0:T(8,128)(2,1)S(1)} %copy-done.15), channel_id=1, replica_groups=mesh['leaf'=64,'panel'=8] {'panel'}, dimensions={0}, use_global_device_ids=true | all-gather | bytes 294912 | tf_op jit(solution)/shard_map/all_gather | solution.py:74
  255.6 20.0 %all_gather.26 = bf16[64,2048]{1,0:T(8,128)(2,1)S(1)} all-gather(bf16[8,2048]{1,0:T(8,128)(2,1)S(1)} %copy-done.16), channel_id=1, replica_groups=mesh['leaf'=64,'panel'=8] {'panel'}, dimensions={0}, use_global_device_ids=true | all-gather | bytes 294912 | tf_op jit(solution)/shard_map/all_gather | solution.py:77
  277.1 14.1 %scatter_fusion.1 = f32[7168,128]{1,0:T(8,128)} fusion(f32[7168,128]{1,0:T(8,128)} %scatter_fusion, s32[2048]{0:T(1024)S(1)} %bitcast.58, f32[2048,128]{1,0:T(8,128)S(1)} %copy.64), kind=kCustom, calls=%fused_computation.5 | custom fusion | flops 262144 | bytes 3153920 | tf_op jit(solution)/shard_map/scatter-add | solution.py:102
  293.0 6.4 collective-permute-start.9
  299.3 20.0 %collective-permute-done.9 = f32[2048,128]{1,0:T(8,128)S(1)} collective-permute-done((f32[2048,128]{1,0:T(8,128)S(1)}, f32[2048,128]{1,0:T(8,128)S(1)}, u32[]{:S(2)}, u32[]{:S(2)}) %collective-permute-start.9) | collective-permute-done | bytes 1048608 | tf_op jit(solution)/shard_map/ppermute | solution.py:13
  321.1 28.8 %collective-permute-start.10 = (f32[1024,128]{1,0:T(8,128)S(1)}, f32[1024,128]{1,0:T(8,128)S(1)}, u32[]{:S(2)}, u32[]{:S(2)}) collective-permute-start(f32[1024,128]{1,0:T(8,128)S(1)} %slice_select_fusion.4), channel_id=1, source_target_pairs={{0,128},{8,136},{16,144},{24,152},{32,160},{40,168},{48,176},{56,1... | collective-permute-start | bytes 1572872 | tf_op jit(solution)/shard_map/ppermute | solution.py:13
  349.9 22.6 %collective-permute-done.10 = f32[1024,128]{1,0:T(8,128)S(1)} collective-permute-done((f32[1024,128]{1,0:T(8,128)S(1)}, f32[1024,128]{1,0:T(8,128)S(1)}, u32[]{:S(2)}, u32[]{:S(2)}) %collective-permute-start.10) | collective-permute-done | bytes 524320 | tf_op jit(solution)/shard_map/ppermute | solution.py:13
  374.5 7.3 collective-permute-done.11
  383.9 5.3 collective-permute-done.12
  394.2 5.6 collective-permute-start.14
  401.9 6.7 all-to-all-start.3
  408.7 22.0 %all_gather.27 = bf16[64,4096]{1,0:T(8,128)(2,1)S(1)} all-gather(bf16[8,4096]{1,0:T(8,128)(2,1)S(1)} %copy-done.12), channel_id=1, replica_groups=mesh['leaf'=64,'panel'=8] {'panel'}, dimensions={0}, use_global_device_ids=true | all-gather | bytes 589824 | tf_op jit(solution)/shard_map/all_gather | solution.py:73
  430.7 6.1 all-to-all-done.3
  443.6 37.0 %collective-permute-done.15 = f32[2048,128]{1,0:T(8,128)S(1)} collective-permute-done((f32[2048,128]{1,0:T(8,128)S(1)}, f32[2048,128]{1,0:T(8,128)S(1)}, u32[]{:S(2)}, u32[]{:S(2)}) %collective-permute-start.15) | collective-permute-done | bytes 1048608 | tf_op jit(solution)/shard_map/ppermute | solution.py:13
  480.9 13.5 %collective-permute-start.16 = (f32[1024,128]{1,0:T(8,128)S(1)}, f32[1024,128]{1,0:T(8,128)S(1)}, u32[]{:S(2)}, u32[]{:S(2)}) collective-permute-start(f32[1024,128]{1,0:T(8,128)S(1)} %slice_select_fusion.3), channel_id=1, source_target_pairs={{0,128},{8,136},{16,144},{24,152},{32,160},{40,168},{48,176},{56,1... | collective-permute-start | bytes 1572872 | tf_op jit(solution)/shard_map/ppermute | solution.py:13
  494.4 21.5 %collective-permute-done.16 = f32[1024,128]{1,0:T(8,128)S(1)} collective-permute-done((f32[1024,128]{1,0:T(8,128)S(1)}, f32[1024,128]{1,0:T(8,128)S(1)}, u32[]{:S(2)}, u32[]{:S(2)}) %collective-permute-start.16) | collective-permute-done | bytes 524320 | tf_op jit(solution)/shard_map/ppermute | solution.py:13
  516.0 4.5 collective-permute-start.17
  520.5 5.1 collective-permute-done.17
  533.0 7.0 collective-permute-start.19
  541.7 5.3 collective-permute-start.20
  549.1 6.2 all-to-all-start.4
  556.5 27.0 %all-to-all-done.4 = bf16[64,64,128]{2,1,0:T(8,128)(2,1)S(1)} async-done(((bf16[64,64,128]{2,1,0:T(8,128)(2,1)}), bf16[64,64,128]{2,1,0:T(8,128)(2,1)S(1)}, u32[]{:S(2)}, u32[]{:S(2)}) %all-to-all-start.4) | async-done | bytes 1048608 | tf_op jit(solution)/shard_map/all_to_all | solution.py:19
  583.6 8.7 %gather_fusion = bf16[2048,128]{1,0:T(8,128)(2,1)} fusion(bf16[7168,128]{1,0:T(8,128)(2,1)S(1)} %scatter.10, s32[2048]{0:T(1024)} %broadcast_clamp_fusion), kind=kCustom, calls=%fused_computation | custom fusion | bytes 1056768 | tf_op jit(solution)/shard_map/jit(_take)/gather | solution.py:111
  596.7 24.5 %collective-permute-done.21 = f32[1024,128]{1,0:T(8,128)S(1)} collective-permute-done((f32[1024,128]{1,0:T(8,128)S(1)}, f32[1024,128]{1,0:T(8,128)S(1)}, u32[]{:S(2)}, u32[]{:S(2)}) %collective-permute-start.21) | collective-permute-done | bytes 524320 | tf_op jit(solution)/shard_map/ppermute | solution.py:13
  623.2 6.4 collective-permute-done.22
  629.7 4.3 collective-permute-start.23
  642.0 6.5 collective-permute-start.25
  650.6 6.1 all-to-all-start.5
  657.3 27.6 %all-to-all-done.5 = bf16[64,64,128]{2,1,0:T(8,128)(2,1)S(1)} async-done(((bf16[64,64,128]{2,1,0:T(8,128)(2,1)}), bf16[64,64,128]{2,1,0:T(8,128)(2,1)S(1)}, u32[]{:S(2)}, u32[]{:S(2)}) %all-to-all-start.5) | async-done | bytes 1048608 | tf_op jit(solution)/shard_map/all_to_all | solution.py:19
  692.8 5.5 collective-permute-done.26
  710.7 6.2 collective-permute-start.29
  719.0 5.7 all-to-all-start.6
  726.1 26.8 %all-to-all-done.6 = bf16[64,64,128]{2,1,0:T(8,128)(2,1)S(1)} async-done(((bf16[64,64,128]{2,1,0:T(8,128)(2,1)}), bf16[64,64,128]{2,1,0:T(8,128)(2,1)S(1)}, u32[]{:S(2)}, u32[]{:S(2)}) %all-to-all-start.6) | async-done | bytes 1048608 | tf_op jit(solution)/shard_map/all_to_all | solution.py:19
  768.0 5.4 collective-permute-start.32
  (195 shorter events, 141.1 us)
Async XLA Ops:
  2.6 58.7 %all-to-all-start = ((bf16[64,64,128]{2,1,0:T(8,128)(2,1)}), bf16[64,64,128]{2,1,0:T(8,128)(2,1)S(1)}, u32[]{:S(2)}, u32[]{:S(2)}) async-start(bf16[64,64,128]{2,1,0:T(8,128)(2,1)} %stack.14), calls=%async_computation | async-start | bytes 2097152 | tf_op jit(solution)/shard_map/all_to_all | solution.py:19
  66.7 50.0 %copy-start.18 = (bf16[8,1024]{1,0:T(8,128)(2,1)S(1)}, bf16[8,1024]{1,0:T(8,128)(2,1)}, u32[]{:S(2)}) copy-start(bf16[8,1024]{1,0:T(8,128)(2,1)} %param.26) | copy-start | bytes 49156
  66.7 70.3 %copy-start.19 = (bf16[8,1024]{1,0:T(8,128)(2,1)S(1)}, bf16[8,1024]{1,0:T(8,128)(2,1)}, u32[]{:S(2)}) copy-start(bf16[8,1024]{1,0:T(8,128)(2,1)} %param.29) | copy-start | bytes 49156
  67.8 7.1 collective-permute-start
  76.0 7.2 collective-permute-start.1
  83.3 5.0 collective-permute-start.2
  88.3 16.8 %collective-permute-start.3 = (f32[64,128]{1,0:T(8,128)S(1)}, f32[64,128]{1,0:T(8,128)S(1)}, u32[]{:S(2)}, u32[]{:S(2)}) collective-permute-start(f32[64,128]{1,0:T(8,128)S(1)} %slice_select_fusion.32), channel_id=1, source_target_pairs={{0,8},{8,0},{16,24},{24,16},{32,40},{40,32},{48,56},{56,48},{64,72... | collective-permute-start | bytes 98312 | tf_op jit(solution)/shard_map/ppermute | solution.py:13
  106.4 51.0 %all-to-all-start.1 = ((bf16[64,64,128]{2,1,0:T(8,128)(2,1)}), bf16[64,64,128]{2,1,0:T(8,128)(2,1)S(1)}, u32[]{:S(2)}, u32[]{:S(2)}) async-start(bf16[64,64,128]{2,1,0:T(8,128)(2,1)} %stack.15), calls=%async_computation.1 | async-start | bytes 2097152 | tf_op jit(solution)/shard_map/all_to_all | solution.py:19
  167.3 57.4 %copy-start.22 = (bf16[64,128]{1,0:T(8,128)(2,1)S(1)}, bf16[64,128]{1,0:T(8,128)(2,1)}, u32[]{:S(2)}) copy-start(bf16[64,128]{1,0:T(8,128)(2,1)} %param.21) | copy-start | bytes 49156
  168.6 22.9 %collective-permute-start.4 = (f32[1024,128]{1,0:T(8,128)S(1)}, f32[1024,128]{1,0:T(8,128)S(1)}, u32[]{:S(2)}, u32[]{:S(2)}) collective-permute-start(f32[1024,128]{1,0:T(8,128)S(1)} %slice_select_fusion.5), channel_id=1, source_target_pairs={{0,128},{8,136},{16,144},{24,152},{32,160},{40,168},{48,176},{56,1... | collective-permute-start | bytes 1572872 | tf_op jit(solution)/shard_map/ppermute | solution.py:13
  192.8 62.8 %copy-start.16 = (bf16[8,2048]{1,0:T(8,128)(2,1)S(1)}, bf16[8,2048]{1,0:T(8,128)(2,1)}, u32[]{:S(2)}) copy-start(bf16[8,2048]{1,0:T(8,128)(2,1)} %param.28) | copy-start | bytes 98308
  192.9 82.8 %copy-start.25 = (s32[2,2048]{1,0:T(2,128)S(1)}, s32[2,2048]{1,0:T(2,128)}, u32[]{:S(2)}) copy-start(s32[2,2048]{1,0:T(2,128)} %param.31) | copy-start | bytes 49156
  192.9 7.1 collective-permute-start.5
  200.1 7.3 collective-permute-start.6
  207.4 5.0 collective-permute-start.7
  212.4 12.3 %collective-permute-start.8 = (f32[64,128]{1,0:T(8,128)S(1)}, f32[64,128]{1,0:T(8,128)S(1)}, u32[]{:S(2)}, u32[]{:S(2)}) collective-permute-start(f32[64,128]{1,0:T(8,128)S(1)} %slice_select_fusion.31), channel_id=1, source_target_pairs={{0,8},{8,0},{16,24},{24,16},{32,40},{40,32},{48,56},{56,48},{64,72... | collective-permute-start | bytes 98312 | tf_op jit(solution)/shard_map/ppermute | solution.py:13
  226.0 50.2 %all-to-all-start.2 = ((bf16[64,64,128]{2,1,0:T(8,128)(2,1)}), bf16[64,64,128]{2,1,0:T(8,128)(2,1)S(1)}, u32[]{:S(2)}, u32[]{:S(2)}) async-start(bf16[64,64,128]{2,1,0:T(8,128)(2,1)} %stack.16), calls=%async_computation.2 | async-start | bytes 2097152 | tf_op jit(solution)/shard_map/all_to_all | solution.py:19
  293.0 26.4 %collective-permute-start.9 = (f32[2048,128]{1,0:T(8,128)S(1)}, f32[2048,128]{1,0:T(8,128)S(1)}, u32[]{:S(2)}, u32[]{:S(2)}) collective-permute-start(f32[2048,128]{1,0:T(8,128)S(1)} %slice_select_fusion.1), channel_id=1, source_target_pairs={{0,256},{8,264},{16,272},{24,280},{32,288},{40,296},{48,304},{56,3... | collective-permute-start | bytes 3145736 | tf_op jit(solution)/shard_map/ppermute | solution.py:13
  321.0 79.6 %copy-start.23 = (bf16[64,128]{1,0:T(8,128)(2,1)S(1)}, bf16[64,128]{1,0:T(8,128)(2,1)}, u32[]{:S(2)}) copy-start(bf16[64,128]{1,0:T(8,128)(2,1)} %param.20) | copy-start | bytes 49156
  321.1 51.4 %collective-permute-start.10 = (f32[1024,128]{1,0:T(8,128)S(1)}, f32[1024,128]{1,0:T(8,128)S(1)}, u32[]{:S(2)}, u32[]{:S(2)}) collective-permute-start(f32[1024,128]{1,0:T(8,128)S(1)} %slice_select_fusion.4), channel_id=1, source_target_pairs={{0,128},{8,136},{16,144},{24,152},{32,160},{40,168},{48,176},{56,1... | collective-permute-start | bytes 1572872 | tf_op jit(solution)/shard_map/ppermute | solution.py:13
  372.6 9.3 %collective-permute-start.11 = (f32[512,128]{1,0:T(8,128)S(1)}, f32[512,128]{1,0:T(8,128)S(1)}, u32[]{:S(2)}, u32[]{:S(2)}) collective-permute-start(f32[512,128]{1,0:T(8,128)S(1)} %slice_select_fusion.9), channel_id=1, source_target_pairs={{0,64},{8,72},{16,80},{24,88},{32,96},{40,104},{48,112},{56,120},{... | collective-permute-start | bytes 786440 | tf_op jit(solution)/shard_map/ppermute | solution.py:13
  381.9 7.2 collective-permute-start.12
  389.2 5.0 collective-permute-start.13
  394.2 6.4 collective-permute-start.14
  401.9 34.9 %all-to-all-start.3 = ((bf16[64,64,128]{2,1,0:T(8,128)(2,1)}), bf16[64,64,128]{2,1,0:T(8,128)(2,1)S(1)}, u32[]{:S(2)}, u32[]{:S(2)}) async-start(bf16[64,64,128]{2,1,0:T(8,128)(2,1)} %stack.17), calls=%async_computation.3 | async-start | bytes 2097152 | tf_op jit(solution)/shard_map/all_to_all | solution.py:19
  439.9 40.7 %collective-permute-start.15 = (f32[2048,128]{1,0:T(8,128)S(1)}, f32[2048,128]{1,0:T(8,128)S(1)}, u32[]{:S(2)}, u32[]{:S(2)}) collective-permute-start(f32[2048,128]{1,0:T(8,128)S(1)} %slice_select_fusion), channel_id=1, source_target_pairs={{0,256},{8,264},{16,272},{24,280},{32,288},{40,296},{48,304},{56,3... | collective-permute-start | bytes 3145736 | tf_op jit(solution)/shard_map/ppermute | solution.py:13
  480.9 35.0 %collective-permute-start.16 = (f32[1024,128]{1,0:T(8,128)S(1)}, f32[1024,128]{1,0:T(8,128)S(1)}, u32[]{:S(2)}, u32[]{:S(2)}) collective-permute-start(f32[1024,128]{1,0:T(8,128)S(1)} %slice_select_fusion.3), channel_id=1, source_target_pairs={{0,128},{8,136},{16,144},{24,152},{32,160},{40,168},{48,176},{56,1... | collective-permute-start | bytes 1572872 | tf_op jit(solution)/shard_map/ppermute | solution.py:13
  516.0 9.6 %collective-permute-start.17 = (f32[512,128]{1,0:T(8,128)S(1)}, f32[512,128]{1,0:T(8,128)S(1)}, u32[]{:S(2)}, u32[]{:S(2)}) collective-permute-start(f32[512,128]{1,0:T(8,128)S(1)} %slice_select_fusion.8), channel_id=1, source_target_pairs={{0,64},{8,72},{16,80},{24,88},{32,96},{40,104},{48,112},{56,120},{... | collective-permute-start | bytes 786440 | tf_op jit(solution)/shard_map/ppermute | solution.py:13
  525.7 7.2 collective-permute-start.18
  533.0 8.7 %collective-permute-start.19 = (f32[128,128]{1,0:T(8,128)S(1)}, f32[128,128]{1,0:T(8,128)S(1)}, u32[]{:S(2)}, u32[]{:S(2)}) collective-permute-start(f32[128,128]{1,0:T(8,128)S(1)} %slice_select_fusion.22), channel_id=1, source_target_pairs={{0,16},{8,24},{16,0},{24,8},{32,48},{40,56},{48,32},{56,40},{64,80... | collective-permute-start | bytes 196616 | tf_op jit(solution)/shard_map/ppermute | solution.py:13
  541.7 6.1 collective-permute-start.20
  549.1 34.3 %all-to-all-start.4 = ((bf16[64,64,128]{2,1,0:T(8,128)(2,1)}), bf16[64,64,128]{2,1,0:T(8,128)(2,1)S(1)}, u32[]{:S(2)}, u32[]{:S(2)}) async-start(bf16[64,64,128]{2,1,0:T(8,128)(2,1)} %stack.18), calls=%async_computation.4 | async-start | bytes 2097152 | tf_op jit(solution)/shard_map/all_to_all | solution.py:19
  594.2 26.9 %collective-permute-start.21 = (f32[1024,128]{1,0:T(8,128)S(1)}, f32[1024,128]{1,0:T(8,128)S(1)}, u32[]{:S(2)}, u32[]{:S(2)}) collective-permute-start(f32[1024,128]{1,0:T(8,128)S(1)} %slice_select_fusion.2), channel_id=1, source_target_pairs={{0,128},{8,136},{16,144},{24,152},{32,160},{40,168},{48,176},{56,1... | collective-permute-start | bytes 1572872 | tf_op jit(solution)/shard_map/ppermute | solution.py:13
  621.3 8.3 %collective-permute-start.22 = (f32[512,128]{1,0:T(8,128)S(1)}, f32[512,128]{1,0:T(8,128)S(1)}, u32[]{:S(2)}, u32[]{:S(2)}) collective-permute-start(f32[512,128]{1,0:T(8,128)S(1)} %slice_select_fusion.7), channel_id=1, source_target_pairs={{0,64},{8,72},{16,80},{24,88},{32,96},{40,104},{48,112},{56,120},{... | collective-permute-start | bytes 786440 | tf_op jit(solution)/shard_map/ppermute | solution.py:13
  629.7 7.2 collective-permute-start.23
  636.9 5.0 collective-permute-start.24
  642.0 7.4 collective-permute-start.25
  650.6 34.3 %all-to-all-start.5 = ((bf16[64,64,128]{2,1,0:T(8,128)(2,1)}), bf16[64,64,128]{2,1,0:T(8,128)(2,1)S(1)}, u32[]{:S(2)}, u32[]{:S(2)}) async-start(bf16[64,64,128]{2,1,0:T(8,128)(2,1)} %stack.19), calls=%async_computation.5 | async-start | bytes 2097152 | tf_op jit(solution)/shard_map/all_to_all | solution.py:19
  689.7 64.6 %copy-start.6 = (bf16[128,64]{0,1:T(8,128)(2,1)S(1)}, bf16[128,64]{0,1:T(8,128)(2,1)}, u32[]{:S(2)}) copy-start(bf16[128,64]{0,1:T(8,128)(2,1)} %copy-done.5) | copy-start | bytes 49156
  689.7 8.6 %collective-permute-start.26 = (f32[512,128]{1,0:T(8,128)S(1)}, f32[512,128]{1,0:T(8,128)S(1)}, u32[]{:S(2)}, u32[]{:S(2)}) collective-permute-start(f32[512,128]{1,0:T(8,128)S(1)} %slice_select_fusion.6), channel_id=1, source_target_pairs={{0,64},{8,72},{16,80},{24,88},{32,96},{40,104},{48,112},{56,120},{... | collective-permute-start | bytes 786440 | tf_op jit(solution)/shard_map/ppermute | solution.py:13
  698.4 7.2 collective-permute-start.27
  705.6 5.0 collective-permute-start.28
  710.7 7.1 collective-permute-start.29
  717.7 57.0 %copy-start.11 = (bf16[64,128]{1,0:T(8,128)(2,1)}, bf16[64,128]{1,0:T(8,128)(2,1)S(1)}, u32[]{:S(2)}) copy-start(bf16[64,128]{1,0:T(8,128)(2,1)S(1)} %add_convert_fusion.1) | copy-start | bytes 49156
  719.0 33.9 %all-to-all-start.6 = ((bf16[64,64,128]{2,1,0:T(8,128)(2,1)}), bf16[64,64,128]{2,1,0:T(8,128)(2,1)S(1)}, u32[]{:S(2)}, u32[]{:S(2)}) async-start(bf16[64,64,128]{2,1,0:T(8,128)(2,1)} %stack.20), calls=%async_computation.6 | async-start | bytes 2097152 | tf_op jit(solution)/shard_map/all_to_all | solution.py:19
  755.7 7.2 collective-permute-start.30
  762.9 5.0 collective-permute-start.31
  768.0 6.2 collective-permute-start.32
  (18 other events, 422.4 us)
